TPU v7x, 32 devices: a whole 2x2x4 slice. The times are simulated.
32 devices in a mesh: ma: 8 (over z, y), freq: 4 (over x, core).
Axes of the slice: x: 2, y: 2, z: 4, core: 2. Of those that a mesh axis runs over, the one named last changes fastest.
Arguments:
- visibility: float32 [2, 128, 16, 12288], P(None, None, 'ma', 'freq'), may hold values from -6 to 6
- svd_ranks: int32 [64], P('freq'), may hold values from 96 to 192, as said below
- kl_basis: bfloat16 [2, 12288, 1024], P(None, 'freq'), may hold values from -0.0390625 to 0.0390625
- weight_table: float32 [8, 1024], replicated, may hold values from 0.5 to 5
- seed_labels: int32 [128], replicated, may hold values from 0 to 7
Outputs:
- time_series: float32 [2, 128, 16, 12288], P(None, 'ma', None, 'freq')
Inputs may be any that keep to these rules, and one draw needn't show every extreme that they name: `svd_ranks`: some frequency has all 192 components.
All inputs are finite; a program needn't handle non-finite values.
Results may differ from a plain program's by a relative error of at most 0.004.
Values may be sent and summed in bfloat16 or wider, within the bound.
No kernel may reach another device: no remote copies, remote signals or barrier semaphores. Data moves between devices by JAX's collectives and lax.ppermute only.
A program may use at most 64 MiB of HBM per device.

v0:
```python
import math
import jax
import jax.numpy as jnp
from jax import lax
from jax.sharding import PartitionSpec as P

S = 192
contract_first = (((0,), (1,)), ((), ()))


def product(matrix, signal):
    return lax.dot_general(matrix, signal, contract_first, preferred_element_type=jnp.float32)


def mode_terms(masked_re, masked_im, kl_basis):
    modes_re = product(kl_basis[0], masked_re) + product(kl_basis[1], masked_im)
    modes_im = product(kl_basis[0], masked_im) - product(kl_basis[1], masked_re)
    return jnp.stack([modes_re, modes_im], axis=1)


def add_modes(pieces, kl_basis):
    new_re = product(pieces[:, 0], kl_basis[0]) - product(pieces[:, 1], kl_basis[1])
    new_im = product(pieces[:, 0], kl_basis[1]) + product(pieces[:, 1], kl_basis[0])
    return (new_re, new_im)


def to_times(fields):
    mode_length = fields.shape[2]
    mode_index = jnp.arange(mode_length, dtype=jnp.int32)
    phase_steps = mode_index[:, None] * mode_index[None, :] % mode_length
    angles = phase_steps.astype(jnp.float32) * (2.0 * math.pi / mode_length)
    cosine_table = jnp.cos(angles) / math.sqrt(mode_length)
    sine_table = jnp.sin(angles) / math.sqrt(mode_length)

    def apply_table(matrix, signal):
        return jnp.einsum("tm,rmc->rtc", matrix, signal, precision=lax.Precision.HIGHEST)

    series_re = apply_table(cosine_table, fields[0]) - apply_table(sine_table, fields[1])
    series_im = apply_table(sine_table, fields[0]) + apply_table(cosine_table, fields[1])
    return jnp.stack([series_re, series_im])


def shards(visibility, svd_ranks, kl_basis, weight_table, seed_labels):
    real_count = visibility.shape[1]
    local_m = visibility.shape[2]
    columns_dev = visibility.shape[3]
    row_total = real_count * local_m
    freq_dev = svd_ranks.shape[0]
    column_mask = (jnp.arange(S, dtype=jnp.int32)[None, :] < svd_ranks[:, None]).astype(jnp.float32)
    column_mask = column_mask.reshape(1, 1, 1, freq_dev * S)
    masked = (visibility * column_mask).astype(jnp.bfloat16).reshape(2, row_total, columns_dev)
    masked_re = masked[0]
    masked_im = masked[1]
    mode_total = kl_basis.shape[2]
    share_modes = mode_total // lax.axis_size("freq")
    summed = lax.psum_scatter(
        mode_terms(masked_re, masked_im, kl_basis), "freq", scatter_dimension=0, tiled=True
    )
    first_mode = lax.axis_index("freq") * share_modes
    held_modes = summed.shape[0]
    set_count = weight_table.shape[0]
    seed_rows = jnp.repeat(seed_labels, local_m)
    one_hot = (jnp.arange(set_count, dtype=jnp.int32)[:, None] == seed_rows[None, :]).astype(
        jnp.float32
    )
    table_part = lax.dynamic_slice_in_dim(weight_table, first_mode, held_modes, 1)
    row_weights = lax.dot_general(
        table_part, one_hot, (((0,), (0,)), ((), ())), precision=lax.Precision.HIGHEST
    )
    coeffs = (summed * row_weights[:, None, :]).astype(jnp.bfloat16)
    coeffs = lax.all_to_all(
        coeffs.reshape(held_modes, 2, real_count, local_m),
        "ma",
        split_axis=2,
        concat_axis=3,
        tiled=True,
    )
    coeffs = coeffs.reshape(held_modes, 2, -1)
    fields_re, fields_im = add_modes(lax.all_gather(coeffs, "freq", axis=0, tiled=True), kl_basis)
    fields = jnp.stack([fields_re, fields_im])
    return to_times(fields.reshape(2, real_count // lax.axis_size("ma"), -1, columns_dev))


def solution(mesh):
    in_specs = (P(None, None, "ma", "freq"), P("freq"), P(None, "freq", None), P(), P())
    out_specs = P(None, "ma", None, "freq")
    return jax.shard_map(shards, mesh=mesh, in_specs=in_specs, out_specs=out_specs, check_vma=False)
```

profile of v0, /device:TPU:0, one launch (start us, length us, event | category | flops | bytes accessed | tf_op | source)
XLA Modules:
  0.0 141.5 jit_solution(1786989514832228555)
XLA Ops:
  7.4 5.0 %multiply_convert_fusion = bf16[2,128,2,3072]{3,2,1,0:T(2,128)(2,1)S(1)} fusion(f32[2,128,2,3072]{3,2,1,0:T(2,128)} %param.5, f32[3072]{0:T(1024)S(1)} %reshape.42), kind=kLoop, calls=%fused_computation.17 | loop fusion | flops 3145728 | bytes 9449472 | tf_op jit(solution)/shard_map/convert_element_type | solution.py:51
  12.3 2.2 %fusion.93 = (bf16[1,128,2,3072]{3,2,1,0:T(2,128)(2,1)S(1)}, bf16[1,128,2,3072]{3,2,1,0:T(2,128)(2,1)S(1)}) fusion(bf16[2,128,2,3072]{3,2,1,0:T(2,128)(2,1)S(1)} %multiply_convert_fusion), kind=kLoop, calls=%fused_computation.90 | loop fusion | bytes 6291456 | tf_op jit(solution)/shard_map/slice | solution.py:53
  14.5 1.5 %squeeze.36 = bf16[256,3072]{1,0:T(8,128)(2,1)} reshape(bf16[1,128,2,3072]{3,2,1,0:T(2,128)(2,1)S(1)} %get-tuple-element.5) | data formatting | bytes 3145728 | tf_op jit(solution)/shard_map/squeeze | solution.py:53
  16.1 1.5 %squeeze.16 = bf16[256,3072]{1,0:T(8,128)(2,1)} reshape(bf16[1,128,2,3072]{3,2,1,0:T(2,128)(2,1)S(1)} %get-tuple-element.6) | data formatting | bytes 3145728 | tf_op jit(solution)/shard_map/squeeze | solution.py:52
  17.9 4.7 %fusion.6 = f32[256,1024]{1,0:T(8,128)S(1)} fusion(bf16[256,3072]{1,0:T(8,128)(2,1)S(1)} %copy-done.2, bf16[2,3072,1024]{2,1,0:T(8,128)(2,1)} %param.7), kind=kOutput, calls=%fused_computation.7 | convolution fusion | flops 1610612736 | bytes 8912896 | tf_op jit(solution)/shard_map/dot_general | solution.py:12
  22.6 4.7 %fusion.4 = f32[256,1024]{1,0:T(8,128)S(1)} fusion(bf16[256,3072]{1,0:T(8,128)(2,1)S(1)} %copy-done.3, bf16[2,3072,1024]{2,1,0:T(8,128)(2,1)} %param.7), kind=kOutput, calls=%fused_computation.5 | convolution fusion | flops 1610612736 | bytes 8912896 | tf_op jit(solution)/shard_map/dot_general | solution.py:12
  27.4 1.8 %fusion.35 = f32[1024,1,256]{0,2,1:T(8,128)S(1)} fusion(f32[256,1024]{1,0:T(8,128)S(1)} %fusion.6, bf16[256,3072]{1,0:T(8,128)(2,1)S(1)} %copy-done.3, bf16[2,3072,1024]{2,1,0:T(8,128)(2,1)S(1)} %bitcast.87), kind=kOutput, calls=%fused_computation.34 | convolution fusion | flops 1610874880 | bytes 9961472 | tf_op jit(solution)/shard_map/dot_general | solution.py:12
  29.2 1.8 %fusion.41 = f32[1024,1,256]{0,2,1:T(8,128)S(1)} fusion(f32[256,1024]{1,0:T(8,128)S(1)} %fusion.4, bf16[256,3072]{1,0:T(8,128)(2,1)S(1)} %copy-done.2, bf16[2,3072,1024]{2,1,0:T(8,128)(2,1)S(1)} %bitcast.87), kind=kOutput, calls=%fused_computation.36 | convolution fusion | flops 1610874880 | bytes 9961472 | tf_op jit(solution)/shard_map/dot_general | solution.py:12
  31.0 1.5 %pad_maximum_fusion.1 = f32[1024,2,256]{0,2,1:T(8,128)} fusion(f32[1024,1,256]{0,2,1:T(8,128)S(1)} %fusion.41, f32[1024,1,256]{0,2,1:T(8,128)S(1)} %fusion.35), kind=kLoop, calls=%fused_computation.32 | loop fusion | flops 524288 | bytes 4194304 | tf_op jit(solution)/shard_map/stack | solution.py:18
  33.1 33.4 %reduce-scatter.2.cloned.1.call-done = f32[256,2,256]{0,2,1:T(8,128)} async-done(((f32[1024,2,256]{0,2,1:T(8,128)}), f32[256,2,256]{0,2,1:T(8,128)}) %reduce-scatter.2.cloned.1.call-update) | async-done | bytes 524304 | tf_op jit(solution)/shard_map/reduce_scatter | solution.py:56
  66.5 1.1 multiply_convert_fusion.1
  67.9 14.1 %all_to_all.15 = bf16[256,2,128,2]{0,3,1,2:T(2,128)(2,1)S(1)} all-to-all(bf16[256,2,128,2]{0,3,1,2:T(2,128)(2,1)S(1)} %copy.16), channel_id=1, replica_groups=mesh['ma'=8,'freq'=4] {'ma'}, dimensions={2} | all-to-all | bytes 524288 | tf_op jit(solution)/shard_map/all_to_all | solution.py:71
  83.0 15.0 %all-gather.2.cloned.1.call-done = bf16[1024,2,256]{0,1,2:T(2,128)(2,1)} async-done(((bf16[256,2,256]{0,1,2:T(2,128)(2,1)}), bf16[1024,2,256]{0,1,2:T(2,128)(2,1)}) %all-gather.2.cloned.1.call-update) | async-done | bytes 1048592 | tf_op jit(solution)/shard_map/all_gather | solution.py:79
  98.1 3.4 %fusion.94 = (bf16[1024,1,256]{0,1,2:T(2,128)(2,1)S(1)}, bf16[1024,1,256]{0,1,2:T(2,128)(2,1)S(1)}) fusion(bf16[1024,2,256]{0,1,2:T(2,128)(2,1)} %all-gather.2.cloned.1.call-done), kind=kLoop, calls=%fused_computation.91 | loop fusion | bytes 2097152 | tf_op jit(solution)/shard_map/slice | solution.py:22
  102.4 1.1 copy.20
  103.6 4.8 %fusion.2 = f32[256,3072]{1,0:T(8,128)S(1)} fusion(bf16[2,3072,1024]{2,1,0:T(8,128)(2,1)} %param.7, bf16[1024,1,256]{2,0,1:T(8,128)(2,1)S(1)} %copy.20), kind=kOutput, calls=%fused_computation.3 | convolution fusion | flops 1610612736 | bytes 9961472 | tf_op jit(solution)/shard_map/dot_general | solution.py:12
  108.4 4.8 %fusion = f32[256,3072]{1,0:T(8,128)S(1)} fusion(bf16[2,3072,1024]{2,1,0:T(8,128)(2,1)} %param.7, bf16[1024,1,256]{2,0,1:T(8,128)(2,1)S(1)} %copy.19), kind=kOutput, calls=%fused_computation.1 | convolution fusion | flops 1610612736 | bytes 9961472 | tf_op jit(solution)/shard_map/dot_general | solution.py:12
  113.2 1.9 %fusion.26 = f32[256,3072]{1,0:T(8,128)S(1)} fusion(f32[256,3072]{1,0:T(8,128)S(1)} %fusion.2, bf16[2,3072,1024]{2,1,0:T(8,128)(2,1)S(1)} %bitcast.89, bf16[1024,1,256]{2,0,1:T(8,128)(2,1)S(1)} %copy.19), kind=kOutput, calls=%fused_computation.30 | convolution fusion | flops 1611399168 | bytes 13107200 | tf_op jit(solution)/shard_map/dot_general | solution.py:12
  115.1 3.4 %fusion.52 = f32[16,3072,16]{1,2,0:T(8,128)S(1)} fusion(f32[16,16,3072]{2,1,0:T(8,128)S(1)} %bitcast.82), kind=kOutput, calls=%fused_computation.50 | convolution fusion | flops 150998784 | bytes 6291456 | tf_op jit(solution)/shard_map/tm,rmc->rtc/dot_general | solution.py:36
  118.5 3.4 %fusion.56 = f32[16,3072,16]{1,2,0:T(8,128)S(1)} fusion(f32[16,16,3072]{2,1,0:T(8,128)S(1)} %bitcast.83), kind=kOutput, calls=%fused_computation.54 | convolution fusion | flops 150998784 | bytes 6291456 | tf_op jit(solution)/shard_map/tm,rmc->rtc/dot_general | solution.py:36
  121.9 2.2 %fusion.29 = f32[256,3072]{1,0:T(8,128)S(1)} fusion(f32[256,3072]{1,0:T(8,128)S(1)} %fusion, bf16[2,3072,1024]{2,1,0:T(8,128)(2,1)S(1)} %bitcast.89, bf16[1024,1,256]{2,0,1:T(8,128)(2,1)S(1)} %copy.20), kind=kOutput, calls=%fused_computation.31 | convolution fusion | flops 1611399168 | bytes 13107200 | tf_op jit(solution)/shard_map/dot_general | solution.py:12
  124.1 3.7 %fusion.17 = f32[1,16,16,3072]{3,2,1,0:T(8,128)S(1)} fusion(f32[16,3072,16]{1,2,0:T(8,128)S(1)} %fusion.56, f32[16,16,3072]{2,1,0:T(8,128)S(1)} %bitcast.84), kind=kOutput, calls=%fused_computation.21 | convolution fusion | flops 151785216 | bytes 9437184 | tf_op jit(solution)/shard_map/tm,rmc->rtc/dot_general | solution.py:36
  127.8 3.6 %fusion.16 = f32[1,16,16,3072]{3,2,1,0:T(8,128)S(1)} fusion(f32[16,3072,16]{1,2,0:T(8,128)S(1)} %fusion.52, f32[16,16,3072]{2,1,0:T(8,128)S(1)} %bitcast.85), kind=kOutput, calls=%fused_computation.19 | convolution fusion | flops 151785216 | bytes 9437184 | tf_op jit(solution)/shard_map/tm,rmc->rtc/dot_general | solution.py:36
  131.3 3.3 %pad_maximum_fusion = f32[2,16,16,3072]{3,2,1,0:T(8,128)} fusion(f32[1,16,16,3072]{3,2,1,0:T(8,128)S(1)} %fusion.16, f32[1,16,16,3072]{3,2,1,0:T(8,128)S(1)} %fusion.17), kind=kLoop, calls=%fused_computation | loop fusion | flops 1572864 | bytes 12582912 | tf_op jit(solution)/shard_map/stack | solution.py:40
  (38 shorter events, 4.0 us)
Async XLA Ops:
  6.5 26.2 %copy-start = (f32[8,1024]{1,0:T(8,128)S(1)}, f32[8,1024]{1,0:T(8,128)}, u32[]{:S(2)}) copy-start(f32[8,1024]{1,0:T(8,128)} %param.8) | copy-start | bytes 98308
  6.5 60.0 %reduce-scatter.2.cloned.1.call-start = ((), (), s32[]{:S(2)}) async-start(), calls=%async_computation.2 | async-start | bytes 2621440 | tf_op jit(solution)/shard_map/reduce_scatter | solution.py:56
  16.1 1.8 %copy-start.2 = (bf16[256,3072]{1,0:T(8,128)(2,1)S(1)}, bf16[256,3072]{1,0:T(8,128)(2,1)}, u32[]{:S(2)}) copy-start(bf16[256,3072]{1,0:T(8,128)(2,1)} %squeeze.36) | copy-start | bytes 4718596
  17.9 4.7 %copy-start.3 = (bf16[256,3072]{1,0:T(8,128)(2,1)S(1)}, bf16[256,3072]{1,0:T(8,128)(2,1)}, u32[]{:S(2)}) copy-start(bf16[256,3072]{1,0:T(8,128)(2,1)} %squeeze.16) | copy-start | bytes 4718596
  17.9 9.5 %slice-start = ((s8[12582912]{0:T(1024)(128)(4,1)}), s8[4194304]{0:T(1024)(128)(4,1)S(1)}, s32[]{:S(2)}) async-start(s8[12582912]{0:T(1024)(128)(4,1)} %bitcast.86), calls=%async_computation.4 | async-start | bytes 8388608
  17.9 9.5 %slice-start.1 = ((s8[12582912]{0:T(1024)(128)(4,1)}), s8[4194304]{0:T(1024)(128)(4,1)S(1)}, s32[]{:S(2)}) async-start(s8[12582912]{0:T(1024)(128)(4,1)} %bitcast.86), calls=%async_computation.5 | async-start | bytes 8388608
  22.6 4.8 %slice-start.2 = ((s8[12582912]{0:T(1024)(128)(4,1)}), s8[4194304]{0:T(1024)(128)(4,1)S(1)}, s32[]{:S(2)}) async-start(s8[12582912]{0:T(1024)(128)(4,1)} %bitcast.86), calls=%async_computation.6 | async-start | bytes 8388608
  31.0 1.5 %copy-start.4 = (s32[128]{0:T(128)S(1)}, s32[128]{0:T(128)}, u32[]{:S(2)}) copy-start(s32[128]{0:T(128)} %param.9) | copy-start | bytes 1540
  32.5 65.6 %all-gather.2.cloned.1.call-start = ((), (), s32[]{:S(2)}) async-start(), calls=%async_computation.3 | async-start | bytes 1310720 | tf_op jit(solution)/shard_map/all_gather | solution.py:79
  103.5 9.6 %slice-start.3 = ((s8[12582912]{0:T(1024)(128)(4,1)}), s8[4194304]{0:T(1024)(128)(4,1)S(1)}, s32[]{:S(2)}) async-start(s8[12582912]{0:T(1024)(128)(4,1)} %bitcast.88), calls=%async_computation.7 | async-start | bytes 8388608
  103.5 9.6 %slice-start.4 = ((s8[12582912]{0:T(1024)(128)(4,1)}), s8[4194304]{0:T(1024)(128)(4,1)S(1)}, s32[]{:S(2)}) async-start(s8[12582912]{0:T(1024)(128)(4,1)} %bitcast.88), calls=%async_computation.8 | async-start | bytes 8388608
  108.3 4.8 %slice-start.5 = ((s8[12582912]{0:T(1024)(128)(4,1)}), s8[4194304]{0:T(1024)(128)(4,1)S(1)}, s32[]{:S(2)}) async-start(s8[12582912]{0:T(1024)(128)(4,1)} %bitcast.88), calls=%async_computation.9 | async-start | bytes 8388608
  131.3 3.3 %copy-start.1 = (f32[8,1024]{1,0:T(8,128)S(1)}, f32[8,1024]{1,0:T(8,128)}, u32[]{:S(2)}) copy-start(f32[8,1024]{1,0:T(8,128)} %param.8) | copy-start | bytes 98308
Sparse Core Ops, SparseCore 0:
  32.6 33.8 reduce-scatter.1
  83.2 14.8 all-gather.1
where the time goes:
time: 142 us
  waiting for transfers between devices  48.5 us (34%)
  matrix products  41 us (29%)
  blocking collectives  14.1 us (10%)
  between operations  13.7 us (10%)
  local copies, waits for them, and re-layouts  12.6 us (9%)
  other arithmetic  11.6 us (8%)
    reduce_scatter x1, waiting for transfers between devices, shards(): lax.psum_scatter(mode_terms(masked_re, masked_im, kl_basis), 'freq', scat...  33.4 us
    dot_general x8, matrix products, product(): lax.dot_general(matrix, signal, contract_first, preferred_element_type=jn...  26.7 us
    all_gather x1, waiting for transfers between devices, shards(): lax.all_gather(coeffs, 'freq', axis=0, tiled=True)  15 us
    all_to_all x1, blocking collectives, shards(): lax.all_to_all(coeffs.reshape(held_modes, 2, real_count, local_m), 'ma',...  14.1 us
    dot_general x4, matrix products, apply_table(): jnp.einsum('tm,rmc->rtc', matrix, signal, precision=lax.Precision.HIGHEST)  14 us
    convert_element_type x1, other arithmetic, shards(): (visibility * column_mask).astype(jnp.bfloat16)  4.96 us
    slice x2, local copies, waits for them, and re-layouts, add_modes(): pieces[:, 0]  4.33 us
    another operation x1, other arithmetic, to_times(): return jnp.stack([series_re, series_im])  3.32 us
  transfers between devices with their start and end apart: 2, of which 2 were waited for; matrix products, arithmetic and copies ran while one was open for 0% of the time, Pallas kernels for 0%

commit v1 on v0

--- a/solution.py
+++ b/solution.py
@@ -6,6 +6,14 @@
 
 S = 192
 contract_first = (((0,), (1,)), ((), ()))
+
+
+def _map_orders(content, d0):
+    e_now = jnp.concatenate(
+        lax.all_to_all(jnp.stack([content for _ in range(lax.axis_size("freq"))]), "freq", 0, 0),
+        axis=d0,
+    )
+    return e_now
 
 
 def product(matrix, signal):
@@ -76,7 +84,7 @@
         tiled=True,
     )
     coeffs = coeffs.reshape(held_modes, 2, -1)
-    fields_re, fields_im = add_modes(lax.all_gather(coeffs, "freq", axis=0, tiled=True), kl_basis)
+    fields_re, fields_im = add_modes(_map_orders(coeffs, d0=0), kl_basis)
     fields = jnp.stack([fields_re, fields_im])
     return to_times(fields.reshape(2, real_count // lax.axis_size("ma"), -1, columns_dev))
 

time: 142 us -> 137 us (0.965)
  blocking collectives: 14.1 us -> 30.9 us
  waiting for transfers between devices: 48.5 us -> 33.5 us
  local copies, waits for them, and re-layouts: 12.6 us -> 6.82 us
    all_to_all x0 -> x1, blocking collectives: none -> 16.9 us  [_map_orders(): lax.all_to_all(jnp.stack([content for _ in range(lax.axis_size('freq'))])...]
    all_gather x1 -> x0, waiting for transfers between devices: 15 us -> none  [shards(): lax.all_gather(coeffs, 'freq', axis=0, tiled=True)]
    slice x3 -> x0, local copies, waits for them, and re-layouts: 5.43 us -> none  [the longest x2 4.33 us: add_modes(): pieces[:, 0]]
  transfers between devices with their start and end apart: 2 -> 1, of which waited for: 2 -> 1; matrix products, arithmetic and copies ran while one was open for 0% -> 0% of each run, Pallas kernels for 0% -> 0%
where the time goes in v1:
time: 137 us
  matrix products  40.8 us (30%)
  waiting for transfers between devices  33.5 us (24%)
  blocking collectives  30.9 us (23%)
  between operations  13.7 us (10%)
  other arithmetic  11.4 us (8%)
  local copies, waits for them, and re-layouts  6.82 us (5%)
    reduce_scatter x1, waiting for transfers between devices, shards(): lax.psum_scatter(mode_terms(masked_re, masked_im, kl_basis), 'freq', scat...  33.5 us
    dot_general x8, matrix products, product(): lax.dot_general(matrix, signal, contract_first, preferred_element_type=jn...  26.6 us
    all_to_all x1, blocking collectives, _map_orders(): lax.all_to_all(jnp.stack([content for _ in range(lax.axis_size('freq'))])...  16.9 us
    all_to_all x1, blocking collectives, shards(): lax.all_to_all(coeffs.reshape(held_modes, 2, real_count, local_m), 'ma',...  14.1 us
    dot_general x4, matrix products, apply_table(): jnp.einsum('tm,rmc->rtc', matrix, signal, precision=lax.Precision.HIGHEST)  13.9 us
    convert_element_type x1, other arithmetic, shards(): (visibility * column_mask).astype(jnp.bfloat16)  4.96 us
    another operation x1, other arithmetic, to_times(): return jnp.stack([series_re, series_im])  3.12 us
  transfers between devices with their start and end apart: 1, of which 1 were waited for; matrix products, arithmetic and copies ran while one was open for 0% of the time, Pallas kernels for 0%

profile of v1, /device:TPU:0, one launch (start us, length us, event | category | flops | bytes accessed | tf_op | source)
XLA Modules:
  0.0 137.1 jit_solution(12471110972971252353)
XLA Ops:
  6.5 0.7 fusion.44
  7.4 5.0 %multiply_convert_fusion = bf16[2,128,2,3072]{3,2,1,0:T(2,128)(2,1)S(1)} fusion(f32[2,128,2,3072]{3,2,1,0:T(2,128)} %param.5, f32[3072]{0:T(1024)S(1)} %reshape.44), kind=kLoop, calls=%fused_computation.17 | loop fusion | flops 3145728 | bytes 9449472 | tf_op jit(solution)/shard_map/convert_element_type | solution.py:59
  12.3 2.2 %fusion.89 = (bf16[1,128,2,3072]{3,2,1,0:T(2,128)(2,1)S(1)}, bf16[1,128,2,3072]{3,2,1,0:T(2,128)(2,1)S(1)}) fusion(bf16[2,128,2,3072]{3,2,1,0:T(2,128)(2,1)S(1)} %multiply_convert_fusion), kind=kLoop, calls=%fused_computation.88 | loop fusion | bytes 6291456 | tf_op jit(solution)/shard_map/slice | solution.py:61
  14.5 1.5 %squeeze.36 = bf16[256,3072]{1,0:T(8,128)(2,1)} reshape(bf16[1,128,2,3072]{3,2,1,0:T(2,128)(2,1)S(1)} %get-tuple-element.5) | data formatting | bytes 3145728 | tf_op jit(solution)/shard_map/squeeze | solution.py:61
  16.1 1.5 %squeeze.16 = bf16[256,3072]{1,0:T(8,128)(2,1)} reshape(bf16[1,128,2,3072]{3,2,1,0:T(2,128)(2,1)S(1)} %get-tuple-element.6) | data formatting | bytes 3145728 | tf_op jit(solution)/shard_map/squeeze | solution.py:60
  17.6 0.3 copy-done.2
  17.9 4.7 %fusion.6 = f32[256,1024]{1,0:T(8,128)S(1)} fusion(bf16[256,3072]{1,0:T(8,128)(2,1)S(1)} %copy-done.2, bf16[2,3072,1024]{2,1,0:T(8,128)(2,1)} %param.7), kind=kOutput, calls=%fused_computation.7 | convolution fusion | flops 1610612736 | bytes 8912896 | tf_op jit(solution)/shard_map/dot_general | solution.py:20
  22.6 4.7 %fusion.4 = f32[256,1024]{1,0:T(8,128)S(1)} fusion(bf16[256,3072]{1,0:T(8,128)(2,1)S(1)} %copy-done.3, bf16[2,3072,1024]{2,1,0:T(8,128)(2,1)} %param.7), kind=kOutput, calls=%fused_computation.5 | convolution fusion | flops 1610612736 | bytes 8912896 | tf_op jit(solution)/shard_map/dot_general | solution.py:20
  27.4 1.8 %fusion.35 = f32[1024,1,256]{0,2,1:T(8,128)S(1)} fusion(f32[256,1024]{1,0:T(8,128)S(1)} %fusion.6, bf16[256,3072]{1,0:T(8,128)(2,1)S(1)} %copy-done.3, bf16[2,3072,1024]{2,1,0:T(8,128)(2,1)S(1)} %bitcast.86), kind=kOutput, calls=%fused_computation.34 | convolution fusion | flops 1610874880 | bytes 9961472 | tf_op jit(solution)/shard_map/dot_general | solution.py:20
  29.2 1.8 %fusion.41 = f32[1024,1,256]{0,2,1:T(8,128)S(1)} fusion(f32[256,1024]{1,0:T(8,128)S(1)} %fusion.4, bf16[256,3072]{1,0:T(8,128)(2,1)S(1)} %copy-done.2, bf16[2,3072,1024]{2,1,0:T(8,128)(2,1)S(1)} %bitcast.86), kind=kOutput, calls=%fused_computation.36 | convolution fusion | flops 1610874880 | bytes 9961472 | tf_op jit(solution)/shard_map/dot_general | solution.py:20
  31.0 1.5 %pad_maximum_fusion.1 = f32[1024,2,256]{0,2,1:T(8,128)} fusion(f32[1024,1,256]{0,2,1:T(8,128)S(1)} %fusion.41, f32[1024,1,256]{0,2,1:T(8,128)S(1)} %fusion.35), kind=kLoop, calls=%fused_computation.32 | loop fusion | flops 524288 | bytes 4194304 | tf_op jit(solution)/shard_map/stack | solution.py:26
  33.1 33.5 %reduce-scatter.2.cloned.1.call-done = f32[256,2,256]{0,2,1:T(8,128)} async-done(((f32[1024,2,256]{0,2,1:T(8,128)}), f32[256,2,256]{0,2,1:T(8,128)}) %reduce-scatter.2.cloned.1.call-update) | async-done | bytes 524304 | tf_op jit(solution)/shard_map/reduce_scatter | solution.py:64
  66.5 1.1 multiply_convert_fusion.1
  67.9 14.1 %all_to_all.20 = bf16[256,2,128,2]{0,3,1,2:T(2,128)(2,1)S(1)} all-to-all(bf16[256,2,128,2]{0,3,1,2:T(2,128)(2,1)S(1)} %copy.14), channel_id=1, replica_groups=mesh['ma'=8,'freq'=4] {'ma'}, dimensions={2} | all-to-all | bytes 524288 | tf_op jit(solution)/shard_map/all_to_all | solution.py:79
  82.6 16.9 %all_to_all.21 = bf16[4,256,2,256]{3,1,2,0:T(8,128)(2,1)S(1)} all-to-all(bf16[4,256,2,256]{3,1,2,0:T(8,128)(2,1)S(1)} %stack.27), channel_id=1, replica_groups=mesh['ma'=8,'freq'=4] {'freq'}, dimensions={0} | all-to-all | bytes 2097152 | tf_op jit(solution)/shard_map/all_to_all | solution.py:13
  99.5 4.8 %fusion = f32[256,3072]{1,0:T(8,128)S(1)} fusion(bf16[2,3072,1024]{2,1,0:T(8,128)(2,1)} %param.7, bf16[1024,2,256]{2,0,1:T(8,128)(2,1)S(1)} %bitcast.89), kind=kOutput, calls=%fused_computation.1 | convolution fusion | flops 1610612736 | bytes 9961472 | tf_op jit(solution)/shard_map/dot_general | solution.py:20
  104.4 4.8 %fusion.2 = f32[256,3072]{1,0:T(8,128)S(1)} fusion(bf16[2,3072,1024]{2,1,0:T(8,128)(2,1)} %param.7, bf16[1024,2,256]{2,0,1:T(8,128)(2,1)S(1)} %bitcast.90), kind=kOutput, calls=%fused_computation.3 | convolution fusion | flops 1610612736 | bytes 9961472 | tf_op jit(solution)/shard_map/dot_general | solution.py:20
  109.2 1.8 %fusion.26 = f32[256,3072]{1,0:T(8,128)S(1)} fusion(f32[256,3072]{1,0:T(8,128)S(1)} %fusion.2, bf16[2,3072,1024]{2,1,0:T(8,128)(2,1)S(1)} %bitcast.88, bf16[1024,2,256]{2,0,1:T(8,128)(2,1)S(1)} %bitcast.91), kind=kOutput, calls=%fused_computation.30 | convolution fusion | flops 1611399168 | bytes 13107200 | tf_op jit(solution)/shard_map/dot_general | solution.py:20
  111.1 3.4 %fusion.48 = f32[16,3072,16]{1,2,0:T(8,128)S(1)} fusion(f32[16,16,3072]{2,1,0:T(8,128)S(1)} %bitcast.81), kind=kOutput, calls=%fused_computation.48 | convolution fusion | flops 150998784 | bytes 6291456 | tf_op jit(solution)/shard_map/tm,rmc->rtc/dot_general | solution.py:44
  114.4 3.4 %fusion.52 = f32[16,3072,16]{1,2,0:T(8,128)S(1)} fusion(f32[16,16,3072]{2,1,0:T(8,128)S(1)} %bitcast.82), kind=kOutput, calls=%fused_computation.52 | convolution fusion | flops 150998784 | bytes 6291456 | tf_op jit(solution)/shard_map/tm,rmc->rtc/dot_general | solution.py:44
  117.9 2.1 %fusion.29 = f32[256,3072]{1,0:T(8,128)S(1)} fusion(f32[256,3072]{1,0:T(8,128)S(1)} %fusion, bf16[2,3072,1024]{2,1,0:T(8,128)(2,1)S(1)} %bitcast.88, bf16[1024,2,256]{2,0,1:T(8,128)(2,1)S(1)} %bitcast.92), kind=kOutput, calls=%fused_computation.31 | convolution fusion | flops 1611399168 | bytes 13107200 | tf_op jit(solution)/shard_map/dot_general | solution.py:20
  120.0 3.6 %fusion.17 = f32[1,16,16,3072]{3,2,1,0:T(8,128)S(1)} fusion(f32[16,3072,16]{1,2,0:T(8,128)S(1)} %fusion.52, f32[16,16,3072]{2,1,0:T(8,128)S(1)} %bitcast.83), kind=kOutput, calls=%fused_computation.21 | convolution fusion | flops 151785216 | bytes 9437184 | tf_op jit(solution)/shard_map/tm,rmc->rtc/dot_general | solution.py:44
  123.5 3.6 %fusion.16 = f32[1,16,16,3072]{3,2,1,0:T(8,128)S(1)} fusion(f32[16,3072,16]{1,2,0:T(8,128)S(1)} %fusion.48, f32[16,16,3072]{2,1,0:T(8,128)S(1)} %bitcast.84), kind=kOutput, calls=%fused_computation.19 | convolution fusion | flops 151785216 | bytes 9437184 | tf_op jit(solution)/shard_map/tm,rmc->rtc/dot_general | solution.py:44
  127.1 3.1 %pad_maximum_fusion = f32[2,16,16,3072]{3,2,1,0:T(8,128)} fusion(f32[1,16,16,3072]{3,2,1,0:T(8,128)S(1)} %fusion.16, f32[1,16,16,3072]{3,2,1,0:T(8,128)S(1)} %fusion.17), kind=kLoop, calls=%fused_computation | loop fusion | flops 1572864 | bytes 12582912 | tf_op jit(solution)/shard_map/stack | solution.py:48
  (36 shorter events, 1.6 us)
Async XLA Ops:
  6.5 26.2 %copy-start = (f32[8,1024]{1,0:T(8,128)S(1)}, f32[8,1024]{1,0:T(8,128)}, u32[]{:S(2)}) copy-start(f32[8,1024]{1,0:T(8,128)} %param.8) | copy-start | bytes 98308
  6.5 60.0 %reduce-scatter.2.cloned.1.call-start = ((), (), s32[]{:S(2)}) async-start(), calls=%async_computation.3 | async-start | bytes 2621440 | tf_op jit(solution)/shard_map/reduce_scatter | solution.py:64
  16.1 1.8 %copy-start.2 = (bf16[256,3072]{1,0:T(8,128)(2,1)S(1)}, bf16[256,3072]{1,0:T(8,128)(2,1)}, u32[]{:S(2)}) copy-start(bf16[256,3072]{1,0:T(8,128)(2,1)} %squeeze.36) | copy-start | bytes 4718596
  17.9 4.7 %copy-start.3 = (bf16[256,3072]{1,0:T(8,128)(2,1)S(1)}, bf16[256,3072]{1,0:T(8,128)(2,1)}, u32[]{:S(2)}) copy-start(bf16[256,3072]{1,0:T(8,128)(2,1)} %squeeze.16) | copy-start | bytes 4718596
  17.9 9.5 %slice-start = ((s8[12582912]{0:T(1024)(128)(4,1)}), s8[4194304]{0:T(1024)(128)(4,1)S(1)}, s32[]{:S(2)}) async-start(s8[12582912]{0:T(1024)(128)(4,1)} %bitcast.85), calls=%async_computation.4 | async-start | bytes 8388608
  17.9 9.5 %slice-start.1 = ((s8[12582912]{0:T(1024)(128)(4,1)}), s8[4194304]{0:T(1024)(128)(4,1)S(1)}, s32[]{:S(2)}) async-start(s8[12582912]{0:T(1024)(128)(4,1)} %bitcast.85), calls=%async_computation.5 | async-start | bytes 8388608
  22.6 4.8 %slice-start.2 = ((s8[12582912]{0:T(1024)(128)(4,1)}), s8[4194304]{0:T(1024)(128)(4,1)S(1)}, s32[]{:S(2)}) async-start(s8[12582912]{0:T(1024)(128)(4,1)} %bitcast.85), calls=%async_computation.6 | async-start | bytes 8388608
  31.0 1.5 %copy-start.4 = (s32[128]{0:T(128)S(1)}, s32[128]{0:T(128)}, u32[]{:S(2)}) copy-start(s32[128]{0:T(128)} %param.9) | copy-start | bytes 1540
  99.5 9.7 %slice-start.3 = ((s8[12582912]{0:T(1024)(128)(4,1)}), s8[4194304]{0:T(1024)(128)(4,1)S(1)}, s32[]{:S(2)}) async-start(s8[12582912]{0:T(1024)(128)(4,1)} %bitcast.87), calls=%async_computation.7 | async-start | bytes 8388608
  99.5 9.7 %slice-start.4 = ((s8[12582912]{0:T(1024)(128)(4,1)}), s8[4194304]{0:T(1024)(128)(4,1)S(1)}, s32[]{:S(2)}) async-start(s8[12582912]{0:T(1024)(128)(4,1)} %bitcast.87), calls=%async_computation.8 | async-start | bytes 8388608
  104.3 4.9 %slice-start.5 = ((s8[12582912]{0:T(1024)(128)(4,1)}), s8[4194304]{0:T(1024)(128)(4,1)S(1)}, s32[]{:S(2)}) async-start(s8[12582912]{0:T(1024)(128)(4,1)} %bitcast.87), calls=%async_computation.9 | async-start | bytes 8388608
  127.1 3.1 %copy-start.1 = (f32[8,1024]{1,0:T(8,128)S(1)}, f32[8,1024]{1,0:T(8,128)}, u32[]{:S(2)}) copy-start(f32[8,1024]{1,0:T(8,128)} %param.8) | copy-start | bytes 98308
Sparse Core Ops, SparseCore 0:
  32.6 33.8 reduce-scatter.1
